TPU v7x, 256 devices: a whole 4x4x8 slice. The times are simulated.
256 devices in a mesh: leaf: 64 (over y, z, core), front: 4 (over x).
Axes of the slice: x: 4, y: 4, z: 8, core: 2. Of those that a mesh axis runs over, the one named last changes fastest.
Arguments:
- rhs_sub: float32 [8, 524288], P(None, ('leaf', 'front')), may hold values from -6 to 6
- rhs_sep: float32 [8, 16384], P(None, 'leaf'), may hold values from -6 to 6
- live_rows: int32 [256], P(('leaf', 'front')), may hold values from 256 to 2048, as said below
- lower_inv: bfloat16 [2048, 256, 256], P(('leaf', 'front')), as said below
- upper_inv: bfloat16 [2048, 256, 256], P(('leaf', 'front'))
- couple_low: bfloat16 [16384, 16384], P(('leaf', 'front')), may hold values from -0.1875 to 0.1875
- couple_up: bfloat16 [16384, 16384], P(('leaf', 'front')), may hold values from -0.046875 to 0.046875
- sep_lower_inv: bfloat16 [16384, 16384], P('leaf', 'front')
- sep_upper_inv: bfloat16 [16384, 16384], P('leaf', 'front')
- basis_sub: float32 [48, 524288], P(None, ('leaf', 'front')), may hold values from -0.0078125 to 0.0078125
- basis_sep: float32 [48, 16384], P(None, 'leaf'), may hold values from -0.0078125 to 0.0078125
Outputs:
- orth_sub: float32 [8, 524288], P(None, ('leaf', 'front'))
- orth_sep: float32 [8, 16384], P(None, 'leaf')
- coef: float32 [48, 8], replicated
Inputs may be any that keep to these rules, and one draw needn't show every extreme that they name: `live_rows`: each entry is a multiple of 256; some device has all 2048 rows live. Every block of lower_inv is lower triangular, and every block of upper_inv, sep_lower_inv and sep_upper_inv upper triangular, each with a diagonal between 1 and 1.5.
All inputs are finite; a program needn't handle non-finite values.
Results may differ from a plain program's by a relative error of at most 0.0055.
Values may be sent and summed in bfloat16 or wider, within the bound.
No kernel may reach another device: no remote copies, remote signals or barrier semaphores. Data moves between devices by JAX's collectives and lax.ppermute only.
A program may use at most 64 MiB of HBM per device.

v0:
```python
import jax
import jax.numpy as jnp
from jax import lax
from jax.sharding import PartitionSpec as P


def apply_blocks(vectors, inverse):
    vec_count = vectors.shape[0]
    shaped = vectors.astype(jnp.bfloat16).reshape(vec_count, inverse.shape[0], inverse.shape[1])
    product = jnp.einsum("vkr,krc->vkc", shaped, inverse, preferred_element_type=jnp.float32)
    return product.reshape(vec_count, inverse.shape[0] * inverse.shape[2])


def shards(
    rhs_sub,
    rhs_sep,
    live_rows,
    lower_inv,
    upper_inv,
    couple_low,
    couple_up,
    sep_lower_inv,
    sep_upper_inv,
    basis_sub,
    basis_sep,
):
    vec_count, row_count = rhs_sub.shape
    border = couple_low.shape[0]
    high = lax.Precision.HIGHEST
    live_mask = lax.broadcasted_iota(jnp.int32, (1, row_count), 1) < live_rows[0]
    lower_sol = jnp.where(live_mask, apply_blocks(rhs_sub, lower_inv), 0.0)
    border_rows = lower_sol[:, :border].astype(jnp.bfloat16)
    columns = couple_low
    top_block = lax.psum_scatter(
        lax.dot_general(
            columns, border_rows, (((0,), (1,)), ((), ())), preferred_element_type=jnp.float32
        ),
        "leaf",
        scatter_dimension=0,
        tiled=True,
    )
    top_block = lax.psum(top_block, "front")
    top_rhs = rhs_sep - top_block.T
    lower_part = jnp.dot(
        top_rhs.astype(jnp.bfloat16), sep_lower_inv, preferred_element_type=jnp.float32
    )
    top_lower = lax.psum(lower_part, "leaf")
    upper_part = lax.dot_general(
        top_lower.astype(jnp.bfloat16),
        sep_upper_inv,
        (((1,), (1,)), ((), ())),
        preferred_element_type=jnp.float32,
    )
    top_sol = lax.psum(upper_part, "front")
    columns = couple_up
    correction = lax.dot_general(
        lax.all_gather(top_sol.astype(jnp.bfloat16), "leaf", axis=1, tiled=True),
        columns,
        (((1,), (1,)), ((), ())),
        preferred_element_type=jnp.float32,
    )
    updated = jnp.concatenate([lower_sol[:, :border] - correction, lower_sol[:, border:]], axis=1)
    upper_sol = jnp.where(live_mask, apply_blocks(updated, upper_inv), 0.0)
    coef_sum = jnp.zeros((basis_sub.shape[0], vec_count), jnp.float32)
    for sweep in range(2):
        local_sub = lax.dot_general(basis_sub, upper_sol, (((1,), (1,)), ((), ())), precision=high)
        local_sep = lax.dot_general(basis_sep, top_sol, (((1,), (1,)), ((), ())), precision=high)
        coef_pass = lax.psum(local_sub, ("leaf", "front")) + lax.psum(local_sep, "leaf")
        part_sub = upper_sol
        part_sep = top_sol
        part_sub = part_sub - lax.dot_general(
            coef_pass, basis_sub, (((0,), (0,)), ((), ())), precision=high
        )
        part_sep = part_sep - lax.dot_general(
            coef_pass, basis_sep, (((0,), (0,)), ((), ())), precision=high
        )
        upper_sol = part_sub
        top_sol = part_sep
        coef_sum = coef_sum + coef_pass
    return (upper_sol, top_sol, coef_sum)


def solution(mesh):
    return jax.shard_map(
        shards,
        mesh=mesh,
        in_specs=(
            P(None, ("leaf", "front")),
            P(None, "leaf"),
            P(("leaf", "front")),
            P(("leaf", "front"), None, None),
            P(("leaf", "front"), None, None),
            P(("leaf", "front"), None),
            P(("leaf", "front"), None),
            P("leaf", "front"),
            P("leaf", "front"),
            P(None, ("leaf", "front")),
            P(None, "leaf"),
        ),
        out_specs=(P(None, ("leaf", "front")), P(None, "leaf"), P()),
        check_vma=False,
    )
```

profile of v0, /device:TPU:0, one launch (start us, length us, event | category | flops | bytes accessed | tf_op | source)
XLA Modules:
  0.0 882.8 jit_solution(9728875847282663332)
XLA Ops:
  7.2 0.0 copy-start
  7.2 0.0 reduce-scatter.2.cloned.1.call-start
  8.0 0.8 convert_element_type.20
  8.9 0.0 copy-start.6
  8.9 1.5 fusion.10
  10.4 0.0 copy-done
  10.4 0.0 copy-start.4
  10.4 1.2 convolution_bitcast_fusion
  11.6 0.0 reduce-scatter.2.cloned.1.call-update
  11.6 0.7 slice.16
  12.3 141.0 %reduce-scatter.2.cloned.1.call-done = f32[256,8]{0,1:T(8,128)} async-done(((f32[16384,8]{0,1:T(8,128)}), f32[256,8]{0,1:T(8,128)}) %reduce-scatter.2.cloned.1.call-update) | async-done | bytes 8208 | tf_op jit(solution)/shard_map/reduce_scatter | solution.py:34
  153.3 0.0 copy-done.4
  153.3 10.6 %psum.49 = f32[8,256]{1,0:T(8,128)S(1)} all-reduce(f32[8,256]{1,0:T(8,128)} %bitcast.49), channel_id=1, replica_groups=mesh['leaf'=64,'front'=4] {'front'}, use_global_device_ids=true, to_apply=%region_1.2 | all-reduce | flops 2048 | bytes 16384 | tf_op jit(solution)/shard_map/psum | solution.py:42
  163.9 0.0 copy-done.6
  163.9 2.0 fusion.6
  165.9 246.2 %all-reduce.1 = bf16[8,4096]{1,0:T(8,128)(2,1)S(1)} all-reduce(f32[8,4096]{1,0:T(8,128)S(1)} %fusion.6), channel_id=1, replica_groups=mesh['leaf'=64,'front'=4] {'leaf'}, use_global_device_ids=true, to_apply=%region_2.3 | all-reduce | flops 32768 | bytes 196608 | tf_op jit(solution)/shard_map/psum | solution.py:47
  412.0 0.0 copy-start.2
  412.0 2.9 fusion.12
  415.0 0.0 copy-start.1
  415.0 7.9 psum.51
  422.9 0.0 copy-start.5
  423.0 41.0 %all_gather.3 = bf16[8,16384]{1,0:T(8,128)(2,1)S(1)} all-gather(bf16[8,256]{1,0:T(8,128)(2,1)S(1)} %convert_element_type.24), channel_id=1, replica_groups=mesh['leaf'=64,'front'=4] {'leaf'}, dimensions={1}, use_global_device_ids=true | all-gather | bytes 266240 | tf_op jit(solution)/shard_map/all_gather | solution.py:57
  463.9 2.2 fusion
  466.2 0.0 copy-done.5
  466.2 0.1 pad_maximum_fusion
  466.3 0.0 copy-done.2
  466.3 0.2 fusion.11
  466.5 0.0 copy-start.3
  466.5 0.6 copy-done.3
  467.2 0.0 copy-done.1
  467.2 0.4 convolution_bitcast_fusion.4
  467.6 75.8 %psum.52 = f32[48,8]{0,1:T(8,128)S(1)} all-reduce(f32[48,8]{0,1:T(8,128)S(1)} %convolution_bitcast_fusion.4), channel_id=1, replica_groups=mesh['leaf'=64,'front'=4] {'leaf','front'}, use_global_device_ids=true, to_apply=%region_4.5 | all-reduce | flops 384 | bytes 3072 | tf_op jit(solution)/shard_map/psum | solution.py:68
  543.4 0.9 convolution_bitcast_fusion.2
  544.4 126.2 %psum.53 = f32[48,8]{0,1:T(8,128)S(1)} all-reduce(f32[48,8]{0,1:T(8,128)S(1)} %convolution_bitcast_fusion.2), channel_id=1, replica_groups=mesh['leaf'=64,'front'=4] {'leaf'}, use_global_device_ids=true, to_apply=%region_5.6 | all-reduce | flops 384 | bytes 3072 | tf_op jit(solution)/shard_map/psum | solution.py:68
  670.6 1.1 convolution_subtract_fusion.1
  671.7 0.9 convolution_subtract_fusion.3
  672.6 0.4 convolution_bitcast_fusion.3
  673.1 71.6 %psum.54 = f32[48,8]{0,1:T(8,128)S(1)} all-reduce(f32[48,8]{0,1:T(8,128)S(1)} %convolution_bitcast_fusion.3), channel_id=1, replica_groups=mesh['leaf'=64,'front'=4] {'leaf','front'}, use_global_device_ids=true, to_apply=%region_6.7 | all-reduce | flops 384 | bytes 3072 | tf_op jit(solution)/shard_map/psum | solution.py:68
  744.7 0.9 convolution_bitcast_fusion.1
  745.6 127.3 %psum.55 = f32[48,8]{0,1:T(8,128)S(1)} all-reduce(f32[48,8]{0,1:T(8,128)S(1)} %convolution_bitcast_fusion.1), channel_id=1, replica_groups=mesh['leaf'=64,'front'=4] {'leaf'}, use_global_device_ids=true, to_apply=%region_7.8 | all-reduce | flops 384 | bytes 3072 | tf_op jit(solution)/shard_map/psum | solution.py:68
  872.9 0.6 add_add_fusion
  873.5 1.5 convolution_subtract_fusion.2
  875.0 0.9 convolution_subtract_fusion
  (4 shorter events, 0.0 us)
Async XLA Ops:
  7.2 3.2 copy-start
  7.2 146.1 %reduce-scatter.2.cloned.1.call-start = ((), (), s32[]{:S(2)}) async-start(), calls=%async_computation.1 | async-start | bytes 532480 | tf_op jit(solution)/shard_map/reduce_scatter | solution.py:34
  8.9 155.0 %copy-start.6 = (f32[8,256]{1,0:T(8,128)S(1)}, f32[8,256]{1,0:T(8,128)}, u32[]{:S(2)}) copy-start(f32[8,256]{1,0:T(8,128)} %param.12) | copy-start | bytes 24580
  10.4 142.9 %copy-start.4 = (f32[8,2048]{1,0:T(8,128)}, f32[8,2048]{1,0:T(8,128)S(1)}, u32[]{:S(2)}) copy-start(f32[8,2048]{1,0:T(8,128)S(1)} %broadcast_select_fusion) | copy-start | bytes 196612
  412.0 54.2 %copy-start.2 = (bf16[8,256,256]{2,1,0:T(8,128)(2,1)S(1)}, bf16[8,256,256]{2,1,0:T(8,128)(2,1)}, u32[]{:S(2)}) copy-start(bf16[8,256,256]{2,1,0:T(8,128)(2,1)} %param.15) | copy-start | bytes 3145732
  415.0 52.2 %copy-start.1 = (f32[48,2048]{1,0:T(8,128)S(1)}, f32[48,2048]{1,0:T(8,128)}, u32[]{:S(2)}) copy-start(f32[48,2048]{1,0:T(8,128)} %param.20) | copy-start | bytes 1179652
  422.9 43.3 %copy-start.5 = (bf16[8,1984]{1,0:T(8,128)(2,1)S(1)}, bf16[8,1984]{1,0:T(8,128)(2,1)}, u32[]{:S(2)}) copy-start(bf16[8,1984]{1,0:T(8,128)(2,1)} %slice.16) | copy-start | bytes 95236
  466.5 0.6 copy-start.3
Sparse Core Ops, SparseCore 0:
  11.9 141.2 reduce-scatter.1
where the time goes:
time: 884 us; the launch traced here: 883 us
  blocking collectives  707 us (80%)
  waiting for transfers between devices  141 us (16%)
  matrix products  17.3 us (2%)
  between operations  14.9 us (2%)
    psum x2, blocking collectives, shards(): lax.psum(local_sep, 'leaf')  253 us
    psum x1, blocking collectives, shards(): top_lower = lax.psum(lower_part, 'leaf')  246 us
    psum x2, blocking collectives, shards(): lax.psum(local_sub, ('leaf', 'front')) + lax.psum(local_sep, 'leaf')  147 us
    reduce_scatter x1, waiting for transfers between devices, shards(): lax.psum_scatter(lax.dot_general(columns, border_rows, (((0,), (1,)), (()...  141 us
    all_gather x1, blocking collectives, shards(): lax.all_gather(top_sol.astype(jnp.bfloat16), 'leaf', axis=1, tiled=True)  41 us
  transfers between devices with their start and end apart: 1, of which 1 were waited for; matrix products, arithmetic and copies ran while one was open for 0% of the time, Pallas kernels for 0%

commit v1 on v0

--- a/solution.py
+++ b/solution.py
@@ -65,7 +65,9 @@
     for sweep in range(2):
         local_sub = lax.dot_general(basis_sub, upper_sol, (((1,), (1,)), ((), ())), precision=high)
         local_sep = lax.dot_general(basis_sep, top_sol, (((1,), (1,)), ((), ())), precision=high)
-        coef_pass = lax.psum(local_sub, ("leaf", "front")) + lax.psum(local_sep, "leaf")
+        coef_pass = jnp.sum(lax.all_gather(local_sub, ("leaf", "front")), axis=0) + lax.psum(
+            local_sep, "leaf"
+        )
         part_sub = upper_sol
         part_sep = top_sol
         part_sub = part_sub - lax.dot_general(

time: 884 us -> 944 us (1.068)
  blocking collectives: 707 us -> 766 us
    all_gather x0 -> x2, blocking collectives: none -> 203 us  [shards(): lax.all_gather(local_sub, ('leaf', 'front'))]
    psum x2 -> x0, blocking collectives: 147 us -> none  [shards(): lax.psum(local_sub, ('leaf', 'front')) + lax.psum(local_sep, 'leaf')]
where the time goes in v1:
time: 944 us; the launch traced here: 943 us
  blocking collectives  766 us (81%)
  waiting for transfers between devices  141 us (15%)
  matrix products  17.3 us (2%)
  between operations  14.9 us (2%)
    psum x2, blocking collectives, shards(): lax.psum(local_sep, 'leaf')  257 us
    psum x1, blocking collectives, shards(): top_lower = lax.psum(lower_part, 'leaf')  246 us
    all_gather x2, blocking collectives, shards(): lax.all_gather(local_sub, ('leaf', 'front'))  203 us
    reduce_scatter x1, waiting for transfers between devices, shards(): lax.psum_scatter(lax.dot_general(columns, border_rows, (((0,), (1,)), (()...  141 us
    all_gather x1, blocking collectives, shards(): lax.all_gather(top_sol.astype(jnp.bfloat16), 'leaf', axis=1, tiled=True)  41 us
  transfers between devices with their start and end apart: 1, of which 1 were waited for; matrix products, arithmetic and copies ran while one was open for 0% of the time, Pallas kernels for 0%

profile of v1, /device:TPU:0, one launch (start us, length us, event | category | flops | bytes accessed | tf_op | source)
XLA Modules:
  0.0 943.4 jit_solution(285065090663142741)
XLA Ops:
  7.2 0.0 copy-start
  7.2 0.0 reduce-scatter.2.cloned.1.call-start
  8.0 0.8 convert_element_type.20
  8.9 0.0 copy-start.10
  8.9 1.5 fusion.10
  10.4 0.0 copy-done
  10.4 0.0 copy-start.6
  10.4 1.2 convolution_bitcast_fusion
  11.6 0.0 reduce-scatter.2.cloned.1.call-update
  11.6 0.7 slice.16
  12.3 141.0 %reduce-scatter.2.cloned.1.call-done = f32[256,8]{0,1:T(8,128)} async-done(((f32[16384,8]{0,1:T(8,128)}), f32[256,8]{0,1:T(8,128)}) %reduce-scatter.2.cloned.1.call-update) | async-done | bytes 8208 | tf_op jit(solution)/shard_map/reduce_scatter | solution.py:34
  153.3 0.0 copy-done.6
  153.3 10.6 %psum.35 = f32[8,256]{1,0:T(8,128)S(1)} all-reduce(f32[8,256]{1,0:T(8,128)} %bitcast.53), channel_id=1, replica_groups=mesh['leaf'=64,'front'=4] {'front'}, use_global_device_ids=true, to_apply=%region_1.2 | all-reduce | flops 2048 | bytes 16384 | tf_op jit(solution)/shard_map/psum | solution.py:42
  163.9 0.0 copy-done.10
  163.9 2.0 fusion.6
  165.9 246.2 %all-reduce.1 = bf16[8,4096]{1,0:T(8,128)(2,1)S(1)} all-reduce(f32[8,4096]{1,0:T(8,128)S(1)} %fusion.6), channel_id=1, replica_groups=mesh['leaf'=64,'front'=4] {'leaf'}, use_global_device_ids=true, to_apply=%region_2.3 | all-reduce | flops 32768 | bytes 196608 | tf_op jit(solution)/shard_map/psum | solution.py:47
  412.0 2.9 fusion.12
  415.0 7.9 psum.37
  422.9 0.0 copy-start.7
  423.0 41.0 %all_gather.15 = bf16[8,16384]{1,0:T(8,128)(2,1)S(1)} all-gather(bf16[8,256]{1,0:T(8,128)(2,1)S(1)} %convert_element_type.24), channel_id=1, replica_groups=mesh['leaf'=64,'front'=4] {'leaf'}, dimensions={1}, use_global_device_ids=true | all-gather | bytes 266240 | tf_op jit(solution)/shard_map/all_gather | solution.py:57
  464.0 2.2 fusion
  466.2 0.0 copy-done.7
  466.2 0.1 pad_maximum_fusion
  466.3 0.0 copy-done.2
  466.3 0.2 fusion.11
  466.5 0.6 copy-done.4
  467.2 0.0 copy-done.1
  467.2 0.4 convolution_bitcast_fusion.4
  467.6 102.5 %all-gather.2 = f32[256,48,8]{1,2,0:T(8,128)S(1)} all-gather(f32[1,48,8]{1,2,0:T(8,128)S(1)} %convolution_bitcast_fusion.4), channel_id=2, replica_groups=mesh['leaf'=64,'front'=4] {'leaf','front'}, dimensions={0}, use_global_device_ids=true | all-gather | bytes 394752 | tf_op jit(solution)/shard_map/all_gather | solution.py:68
  570.1 0.0 copy-done.3
  570.1 0.1 convolution_bitcast_fusion.2
  570.2 128.8 %psum.38 = f32[48,8]{0,1:T(8,128)} all-reduce(f32[48,8]{0,1:T(8,128)S(1)} %convolution_bitcast_fusion.2), channel_id=1, replica_groups=mesh['leaf'=64,'front'=4] {'leaf'}, use_global_device_ids=true, to_apply=%region_5.6 | all-reduce | flops 384 | bytes 3072 | tf_op jit(solution)/shard_map/psum | solution.py:68
  699.1 0.3 reduce_sum.18
  699.3 0.7 add.21
  700.0 1.1 convolution_subtract_fusion.1
  701.2 0.0 copy-start.5
  701.2 1.0 convolution_subtract_fusion.3
  702.2 0.0 copy-done.8
  702.2 0.0 copy-done.5
  702.2 0.4 convolution_bitcast_fusion.3
  702.6 100.6 %all-gather.3 = f32[256,48,8]{1,2,0:T(8,128)S(1)} all-gather(f32[1,48,8]{1,2,0:T(8,128)S(1)} %convolution_bitcast_fusion.3), channel_id=3, replica_groups=mesh['leaf'=64,'front'=4] {'leaf','front'}, dimensions={0}, use_global_device_ids=true | all-gather | bytes 394752 | tf_op jit(solution)/shard_map/all_gather | solution.py:68
  803.2 0.3 reduce_sum.19
  803.5 0.9 convolution_bitcast_fusion.1
  804.4 128.3 %psum.39 = f32[48,8]{0,1:T(8,128)S(1)} all-reduce(f32[48,8]{0,1:T(8,128)S(1)} %convolution_bitcast_fusion.1), channel_id=1, replica_groups=mesh['leaf'=64,'front'=4] {'leaf'}, use_global_device_ids=true, to_apply=%region_7.8 | all-reduce | flops 384 | bytes 3072 | tf_op jit(solution)/shard_map/psum | solution.py:68
  932.7 0.0 copy-done.9
  932.7 0.6 add_add_fusion
  933.3 1.5 convolution_subtract_fusion.2
  934.8 1.8 convolution_subtract_fusion
  (9 shorter events, 0.0 us)
Async XLA Ops:
  7.2 3.2 copy-start
  7.2 146.1 %reduce-scatter.2.cloned.1.call-start = ((), (), s32[]{:S(2)}) async-start(), calls=%async_computation.1 | async-start | bytes 532480 | tf_op jit(solution)/shard_map/reduce_scatter | solution.py:34
  8.9 155.0 %copy-start.10 = (f32[8,256]{1,0:T(8,128)S(1)}, f32[8,256]{1,0:T(8,128)}, u32[]{:S(2)}) copy-start(f32[8,256]{1,0:T(8,128)} %param.12) | copy-start | bytes 24580
  10.4 142.9 %copy-start.6 = (f32[8,2048]{1,0:T(8,128)}, f32[8,2048]{1,0:T(8,128)S(1)}, u32[]{:S(2)}) copy-start(f32[8,2048]{1,0:T(8,128)S(1)} %broadcast_select_fusion) | copy-start | bytes 196612
  412.0 54.2 %copy-start.2 = (bf16[8,256,256]{2,1,0:T(8,128)(2,1)S(1)}, bf16[8,256,256]{2,1,0:T(8,128)(2,1)}, u32[]{:S(2)}) copy-start(bf16[8,256,256]{2,1,0:T(8,128)(2,1)} %param.15) | copy-start | bytes 3145732
  415.0 52.2 %copy-start.1 = (f32[48,2048]{1,0:T(8,128)S(1)}, f32[48,2048]{1,0:T(8,128)}, u32[]{:S(2)}) copy-start(f32[48,2048]{1,0:T(8,128)} %param.20) | copy-start | bytes 1179652
  422.9 43.3 %copy-start.7 = (bf16[8,1984]{1,0:T(8,128)(2,1)S(1)}, bf16[8,1984]{1,0:T(8,128)(2,1)}, u32[]{:S(2)}) copy-start(bf16[8,1984]{1,0:T(8,128)(2,1)} %slice.16) | copy-start | bytes 95236
  463.9 106.2 %copy-start.3 = (f32[48,256]{1,0:T(8,128)S(1)}, f32[48,256]{1,0:T(8,128)}, u32[]{:S(2)}) copy-start(f32[48,256]{1,0:T(8,128)} %param.21) | copy-start | bytes 147460
  466.5 0.6 copy-start.4
  700.0 2.1 copy-start.8
  701.2 1.0 copy-start.5
  702.6 230.1 %copy-start.9 = (f32[48,8]{0,1:T(8,128)S(1)}, f32[48,8]{0,1:T(8,128)}, u32[]{:S(2)}) copy-start(f32[48,8]{0,1:T(8,128)} %copy-done.8) | copy-start | bytes 4612
Sparse Core Ops, SparseCore 0:
  11.9 141.2 reduce-scatter.1

commit v2 on v0

--- a/solution.py
+++ b/solution.py
@@ -65,7 +65,7 @@
     for sweep in range(2):
         local_sub = lax.dot_general(basis_sub, upper_sol, (((1,), (1,)), ((), ())), precision=high)
         local_sep = lax.dot_general(basis_sep, top_sol, (((1,), (1,)), ((), ())), precision=high)
-        coef_pass = lax.psum(local_sub, ("leaf", "front")) + lax.psum(local_sep, "leaf")
+        coef_pass = lax.psum(lax.psum(local_sub, "leaf"), "front") + lax.psum(local_sep, "leaf")
         part_sub = upper_sol
         part_sep = top_sol
         part_sub = part_sub - lax.dot_general(

time: 884 us -> 757 us (0.86)
  blocking collectives: 707 us -> 578 us
    psum x4, blocking collectives: 401 us -> 272 us  [the longest x2 255 us: shards(): lax.psum(local_sub, 'leaf')]
where the time goes in v2:
time: 757 us; the launch traced here: 754 us
  blocking collectives  578 us (76%)
  waiting for transfers between devices  141 us (19%)
  matrix products  17.3 us (2%)
  between operations  14.9 us (2%)
    psum x2, blocking collectives, shards(): lax.psum(local_sub, 'leaf')  255 us
    psum x1, blocking collectives, shards(): top_lower = lax.psum(lower_part, 'leaf')  246 us
    reduce_scatter x1, waiting for transfers between devices, shards(): lax.psum_scatter(lax.dot_general(columns, border_rows, (((0,), (1,)), (()...  141 us
    all_gather x1, blocking collectives, shards(): lax.all_gather(top_sol.astype(jnp.bfloat16), 'leaf', axis=1, tiled=True)  41 us
    psum x2, blocking collectives, shards(): lax.psum(lax.psum(local_sub, 'leaf'), 'front') + lax.psum(local_sep, 'leaf')  17.5 us
  transfers between devices with their start and end apart: 1, of which 1 were waited for; matrix products, arithmetic and copies ran while one was open for 0% of the time, Pallas kernels for 0%

profile of v2, /device:TPU:0, one launch (start us, length us, event | category | flops | bytes accessed | tf_op | source)
XLA Modules:
  0.0 754.4 jit_solution(11164718991153471304)
XLA Ops:
  7.2 0.0 copy-start
  7.2 0.0 reduce-scatter.2.cloned.1.call-start
  8.0 0.8 convert_element_type.20
  8.9 0.0 copy-start.6
  8.9 1.5 fusion.10
  10.4 0.0 copy-done
  10.4 0.0 copy-start.4
  10.4 1.2 convolution_bitcast_fusion
  11.6 0.0 reduce-scatter.2.cloned.1.call-update
  11.6 0.7 slice.16
  12.3 141.0 %reduce-scatter.2.cloned.1.call-done = f32[256,8]{0,1:T(8,128)} async-done(((f32[16384,8]{0,1:T(8,128)}), f32[256,8]{0,1:T(8,128)}) %reduce-scatter.2.cloned.1.call-update) | async-done | bytes 8208 | tf_op jit(solution)/shard_map/reduce_scatter | solution.py:34
  153.3 0.0 copy-done.4
  153.3 10.6 %psum.63 = f32[8,256]{1,0:T(8,128)S(1)} all-reduce(f32[8,256]{1,0:T(8,128)} %bitcast.49), channel_id=1, replica_groups=mesh['leaf'=64,'front'=4] {'front'}, use_global_device_ids=true, to_apply=%region_1.2 | all-reduce | flops 2048 | bytes 16384 | tf_op jit(solution)/shard_map/psum | solution.py:42
  163.9 0.0 copy-done.6
  163.9 2.0 fusion.6
  165.9 246.2 %all-reduce.3 = bf16[8,4096]{1,0:T(8,128)(2,1)S(1)} all-reduce(f32[8,4096]{1,0:T(8,128)S(1)} %fusion.6), channel_id=1, replica_groups=mesh['leaf'=64,'front'=4] {'leaf'}, use_global_device_ids=true, to_apply=%region_2.3 | all-reduce | flops 32768 | bytes 196608 | tf_op jit(solution)/shard_map/psum | solution.py:47
  412.0 0.0 copy-start.2
  412.0 2.9 fusion.12
  415.0 0.0 copy-start.1
  415.0 7.9 %psum.65 = f32[8,256]{1,0:T(8,128)S(1)} all-reduce(f32[8,256]{1,0:T(8,128)} %fusion.12), channel_id=1, replica_groups=mesh['leaf'=64,'front'=4] {'front'}, use_global_device_ids=true, to_apply=%region_3.4 | all-reduce | flops 2048 | bytes 16384 | tf_op jit(solution)/shard_map/psum | solution.py:54
  422.9 0.0 copy-start.5
  423.0 41.0 %all_gather.3 = bf16[8,16384]{1,0:T(8,128)(2,1)S(1)} all-gather(bf16[8,256]{1,0:T(8,128)(2,1)S(1)} %convert_element_type.24), channel_id=1, replica_groups=mesh['leaf'=64,'front'=4] {'leaf'}, dimensions={1}, use_global_device_ids=true | all-gather | bytes 266240 | tf_op jit(solution)/shard_map/all_gather | solution.py:57
  463.9 0.9 convolution_bitcast_fusion.2
  464.9 2.3 fusion
  467.1 0.0 copy-done.5
  467.1 0.1 pad_maximum_fusion
  467.2 0.0 copy-done.2
  467.2 0.2 fusion.11
  467.5 0.0 copy-start.3
  467.5 0.6 copy-done.3
  468.1 0.0 copy-done.1
  468.1 0.4 convolution_bitcast_fusion.4
  468.5 128.8 %all-reduce.1 = (f32[48,8]{0,1:T(8,128)S(1)}, f32[48,8]{0,1:T(8,128)S(1)}) all-reduce(f32[48,8]{0,1:T(8,128)S(1)} %convolution_bitcast_fusion.4, f32[48,8]{0,1:T(8,128)S(1)} %convolution_bitcast_fusion.2), channel_id=1, replica_groups=mesh['leaf'=64,'front'=4] {'leaf'}, use_global_device_ids=true, to_apply=%region_4.5 | all-reduce | flops 768 | bytes 6144 | tf_op jit(solution)/shard_map/psum | solution.py:68
  597.4 9.8 %psum.67 = f32[48,8]{0,1:T(8,128)S(1)} all-reduce(f32[48,8]{0,1:T(8,128)S(1)} %get-tuple-element.5), channel_id=1, replica_groups=mesh['leaf'=64,'front'=4] {'front'}, use_global_device_ids=true, to_apply=%region_5.6 | all-reduce | flops 384 | bytes 3072 | tf_op jit(solution)/shard_map/psum | solution.py:68
  607.1 1.1 convolution_subtract_fusion.1
  608.3 0.9 convolution_subtract_fusion.3
  609.2 0.4 convolution_bitcast_fusion.3
  609.6 1.0 convolution_bitcast_fusion.1
  610.6 126.1 %all-reduce = (f32[48,8]{0,1:T(8,128)S(1)}, f32[48,8]{0,1:T(8,128)S(1)}) all-reduce(f32[48,8]{0,1:T(8,128)S(1)} %convolution_bitcast_fusion.3, f32[48,8]{0,1:T(8,128)S(1)} %convolution_bitcast_fusion.1), channel_id=1, replica_groups=mesh['leaf'=64,'front'=4] {'leaf'}, use_global_device_ids=true, to_apply=%region_7.8 | all-reduce | flops 768 | bytes 6144 | tf_op jit(solution)/shard_map/psum | solution.py:68
  736.7 7.8 %psum.70 = f32[48,8]{0,1:T(8,128)S(1)} all-reduce(f32[48,8]{0,1:T(8,128)S(1)} %get-tuple-element.3), channel_id=1, replica_groups=mesh['leaf'=64,'front'=4] {'front'}, use_global_device_ids=true, to_apply=%region_8.9 | all-reduce | flops 384 | bytes 3072 | tf_op jit(solution)/shard_map/psum | solution.py:68
  744.4 0.6 add_add_fusion
  745.0 1.5 convolution_subtract_fusion.2
  746.6 0.9 convolution_subtract_fusion
  (4 shorter events, 0.0 us)
Async XLA Ops:
  7.2 3.2 copy-start
  7.2 146.1 %reduce-scatter.2.cloned.1.call-start = ((), (), s32[]{:S(2)}) async-start(), calls=%async_computation.1 | async-start | bytes 532480 | tf_op jit(solution)/shard_map/reduce_scatter | solution.py:34
  8.9 155.0 %copy-start.6 = (f32[8,256]{1,0:T(8,128)S(1)}, f32[8,256]{1,0:T(8,128)}, u32[]{:S(2)}) copy-start(f32[8,256]{1,0:T(8,128)} %param.12) | copy-start | bytes 24580
  10.4 142.9 %copy-start.4 = (f32[8,2048]{1,0:T(8,128)}, f32[8,2048]{1,0:T(8,128)S(1)}, u32[]{:S(2)}) copy-start(f32[8,2048]{1,0:T(8,128)S(1)} %broadcast_select_fusion) | copy-start | bytes 196612
  412.0 55.2 %copy-start.2 = (bf16[8,256,256]{2,1,0:T(8,128)(2,1)S(1)}, bf16[8,256,256]{2,1,0:T(8,128)(2,1)}, u32[]{:S(2)}) copy-start(bf16[8,256,256]{2,1,0:T(8,128)(2,1)} %param.15) | copy-start | bytes 3145732
  415.0 53.2 %copy-start.1 = (f32[48,2048]{1,0:T(8,128)S(1)}, f32[48,2048]{1,0:T(8,128)}, u32[]{:S(2)}) copy-start(f32[48,2048]{1,0:T(8,128)} %param.20) | copy-start | bytes 1179652
  422.9 44.2 %copy-start.5 = (bf16[8,1984]{1,0:T(8,128)(2,1)S(1)}, bf16[8,1984]{1,0:T(8,128)(2,1)}, u32[]{:S(2)}) copy-start(bf16[8,1984]{1,0:T(8,128)(2,1)} %slice.16) | copy-start | bytes 95236
  467.5 0.6 copy-start.3
Sparse Core Ops, SparseCore 0:
  11.9 141.2 reduce-scatter.1
